TPU v7x, 32 devices: a whole 2x2x4 slice. The times are simulated.
32 devices in a mesh: groups: 2 (over x), img: 16 (over z, y, core).
Axes of the slice: x: 2, y: 2, z: 4, core: 2. Of those that a mesh axis runs over, the one named last changes fastest.
Arguments:
- images: bfloat16 [256, 4608], P(('groups', 'img')), parts along dimension 0, may hold values from -64 to 64
- class_refs: bfloat16 [96, 4608], P('groups', 'img'), parts along dimension 0, may hold values from -0.6 to 0.6
- sigma2: float32 [32, 16], P('groups'), parts along dimension 0, may hold values from 0.5 to 18
- ctf_group: int32 [256], P(('groups', 'img')), parts along dimension 0, may hold values from 0 to 15, as said below
- defocus_bin: int32 [256], P(('groups', 'img')), parts along dimension 0, may hold values from 0 to 31
Outputs:
- new_refs: float32 [96, 4608], P('groups', 'img'), parts along dimension 0
There are 2 independent parts, one for each index of `groups`. A program takes and returns all parts, laid end to end along the dimension named above; each array names one. Nothing has to cross between parts.
Inputs may be any that keep to these rules, and one draw needn't show every extreme that they name: `ctf_group`: never falls from one image to the next; every group appears.
All inputs are finite; a program needn't handle non-finite values.
Results may differ from a plain program's by a relative error of at most 0.0084.
Values may be sent and summed in bfloat16 or wider, within the bound.
A program may use at most 128 MiB of HBM per device.

v0:
```python
import math

import jax
import jax.numpy as jnp
from jax import lax
from jax.experimental import pallas as pl
from jax.experimental.pallas import tpu as pltpu
from jax.sharding import PartitionSpec as P

CLASSES = 48
ROT = 36
SHELLS = 16
ANG = 144
REACH = 3
SHIFTS = 49
BINS = 32
NGROUP = 16


def shell_radius():
    return (jnp.arange(SHELLS, dtype=jnp.float32) + 1.0) / (2.0 * SHELLS)


def ctf_table():
    defocus = 1.0 + jnp.arange(BINS, dtype=jnp.float32) / BINS
    radius = shell_radius()
    return -jnp.sin(80.0 * defocus[:, None] * radius[None, :] ** 2 + 0.1)


def angle_major(values):
    count = values.shape[0]
    return (
        values.reshape(count, 2, SHELLS, ANG).transpose(0, 3, 1, 2).reshape(count, 2 * SHELLS * ANG)
    )


def shell_major(values):
    count = values.shape[0]
    return (
        values.reshape(count, ANG, 2, SHELLS).transpose(0, 2, 3, 1).reshape(count, 2 * SHELLS * ANG)
    )


def phase_flat():
    offsets = jnp.arange(2 * REACH + 1, dtype=jnp.float32) - REACH
    shift_x = jnp.repeat(offsets, 2 * REACH + 1)
    shift_y = jnp.tile(offsets, 2 * REACH + 1)
    angles = 2.0 * math.pi * jnp.arange(ANG, dtype=jnp.float32) / ANG
    radius = shell_radius()
    phase = (
        2.0
        * math.pi
        * radius[None, None, :]
        * (
            jnp.cos(angles)[None, :, None] * shift_x[:, None, None]
            + jnp.sin(angles)[None, :, None] * shift_y[:, None, None]
        )
    )
    cosine = jnp.cos(phase)
    sine_table = jnp.sin(phase)
    cos_flat = jnp.stack([cosine, cosine], axis=2).reshape(SHIFTS, 2 * SHELLS * ANG)
    sin_flat = jnp.stack([-sine_table, sine_table], axis=2).reshape(SHIFTS, 2 * SHELLS * ANG)
    return (cos_flat, sin_flat)


def image_weights(ctf_group, defocus_bin, sigma2):
    bin_hot = (defocus_bin[:, None] == jnp.arange(BINS, dtype=jnp.int32)[None, :]).astype(
        jnp.float32
    )
    group_hot = (ctf_group[:, None] == jnp.arange(NGROUP, dtype=jnp.int32)[None, :]).astype(
        jnp.float32
    )
    ctf_sel = jnp.dot(bin_hot, ctf_table(), precision=lax.Precision.HIGHEST)
    noise_sel = jnp.dot(group_hot, sigma2, precision=lax.Precision.HIGHEST)
    return (ctf_sel / noise_sel, ctf_sel * ctf_sel / noise_sel)


LANES = 128
STEP = ANG // ROT
SPAN = STEP * 2 * SHELLS
WIDTH = ROT * SPAN
BIG = 1e30


def fold_lanes(row, count_img, combine):
    cols = row.shape[1]
    total = row[:, :LANES]
    for start in range(LANES, cols, LANES):
        total = combine(total, row[:, start : start + LANES])
    reach = count_img
    while reach < LANES:
        total = combine(total, pltpu.roll(total, reach, 1))
        reach *= 2
    return jnp.concatenate([total] * (cols // LANES), axis=1)


def em_kernel(
    count_img,
    refs_ref,
    img_ref,
    fw_ref,
    cos_ref,
    sin_ref,
    sw_ref,
    num_ref,
    field_ref,
    feats,
    twice,
    scores,
    post,
    acc,
):
    rows = CLASSES
    cols = feats.shape[0]
    used = SHIFTS * count_img
    filtered = img_ref[...].astype(jnp.float32) * jnp.concatenate([fw_ref[...]] * ROT, axis=1)
    lane = lax.broadcasted_iota(jnp.int32, (count_img, WIDTH), 1)
    real_lane = lax.rem(lane, 2 * SHELLS) < SHELLS
    swapped = jnp.where(
        real_lane,
        pltpu.roll(filtered, WIDTH - SHELLS, 1),
        pltpu.roll(filtered, SHELLS, 1),
    )

    def shifted(shift):
        cosine = cos_ref[pl.ds(shift, 1), :]
        sine = sin_ref[pl.ds(shift, 1), :]
        return filtered * cosine + swapped * sine

    def feature_pair(pair, carry):
        first = shifted(2 * pair)
        second = shifted(2 * pair + 1)
        start = pl.multiple_of(pair * 2 * count_img, 2 * count_img)
        feats[pl.ds(start, 2 * count_img), :] = jnp.concatenate([first, second], axis=0).astype(
            jnp.bfloat16
        )
        return carry

    lax.fori_loop(0, SHIFTS // 2, feature_pair, 0)
    last = shifted(SHIFTS - 1)
    feats[used - count_img : used + count_img, :] = jnp.concatenate(
        [last, jnp.zeros_like(last)], axis=0
    ).astype(jnp.bfloat16)
    feats[used + count_img :, :] = jnp.zeros((cols - used - count_img, WIDTH), jnp.bfloat16)

    refs = refs_ref[...]
    twice[:, :WIDTH] = refs
    twice[:, WIDTH:] = refs
    power = jnp.zeros((rows, SPAN), jnp.float32)
    for block in range(ROT):
        piece = refs_ref[:, block * SPAN : (block + 1) * SPAN].astype(jnp.float32)
        power = power + piece * piece
    quad = 0.5 * lax.dot_general(
        power,
        sw_ref[...],
        (((1,), (0,)), ((), ())),
        precision=lax.Precision.HIGHEST,
        preferred_element_type=jnp.float32,
    )
    col = lax.broadcasted_iota(jnp.int32, (rows, cols), 1)
    quad = jnp.where(col < used, quad, BIG)

    depth = 4 * SPAN
    for turn in range(ROT):
        scores[turn * rows : (turn + 1) * rows, :] = -quad

    def cross_step(step, carry):
        base = pl.multiple_of(step * depth, depth)
        left = jnp.concatenate(
            [
                twice[:, pl.ds(pl.multiple_of(base + (ROT - turn) * SPAN, SPAN), depth)]
                for turn in range(ROT)
            ],
            axis=0,
        )
        scores[...] += lax.dot_general(
            left,
            feats[:, pl.ds(base, depth)],
            (((1,), (1,)), ((), ())),
            preferred_element_type=jnp.float32,
        )
        return carry

    lax.fori_loop(0, WIDTH // depth, cross_step, 0)

    def max_step(turn, best):
        start = pl.multiple_of(turn * rows, rows)
        return jnp.maximum(best, scores[pl.ds(start, rows), :])

    best = lax.fori_loop(0, ROT, max_step, jnp.full((rows, cols), -BIG, jnp.float32))
    top = fold_lanes(jnp.max(best, axis=0, keepdims=True), count_img, jnp.maximum)

    def exp_step(turn, total):
        start = pl.multiple_of(turn * rows, rows)
        value = jnp.exp(scores[pl.ds(start, rows), :] - top)
        scores[pl.ds(start, rows), :] = value
        return total + value

    total = lax.fori_loop(0, ROT, exp_step, jnp.zeros((rows, cols), jnp.float32))
    norm = fold_lanes(jnp.sum(total, axis=0, keepdims=True), count_img, jnp.add)
    scale = 1.0 / norm

    def post_step(turn, carry):
        start = pl.multiple_of(turn * rows, rows)
        post[pl.ds(start, rows), :] = (scores[pl.ds(start, rows), :] * scale).astype(jnp.bfloat16)
        return carry

    lax.fori_loop(0, ROT, post_step, 0)
    field_ref[...] = lax.dot_general(
        total * scale,
        sw_ref[...],
        (((1,), (1,)), ((), ())),
        precision=lax.Precision.HIGHEST,
        preferred_element_type=jnp.float32,
    )

    acc[...] = jnp.zeros_like(acc)
    wide = 2 * SPAN

    def back_step(step, carry):
        base = pl.multiple_of(step * wide, wide)
        oriented = jnp.dot(
            post[...], feats[:, pl.ds(base, wide)], preferred_element_type=jnp.float32
        )
        for turn in range(ROT):
            where = pl.ds(pl.multiple_of(base + (ROT - turn) * SPAN, SPAN), wide)
            acc[:, where] += oriented[turn * rows : (turn + 1) * rows]
        return carry

    lax.fori_loop(0, WIDTH // wide, back_step, 0)
    num_ref[...] = acc[:, :WIDTH] + acc[:, WIDTH:]


def em_step(refs_angle, images_angle, filter_weight, shell_weight):
    count_img = images_angle.shape[0]
    cols = -(-(SHIFTS + 1) * count_img // LANES) * LANES
    repeats = SPAN // SHELLS
    cos_flat, sin_flat = phase_flat()
    weight_rows = jnp.pad(jnp.tile(shell_weight.T, (repeats, SHIFTS)), ((0, 0), (0, cols - SHIFTS * count_img)))
    return pl.pallas_call(
        lambda *refs: em_kernel(count_img, *refs),
        out_shape=(
            jax.ShapeDtypeStruct((CLASSES, WIDTH), jnp.float32),
            jax.ShapeDtypeStruct((CLASSES, SPAN), jnp.float32),
        ),
        in_specs=[pl.BlockSpec(memory_space=pltpu.VMEM)] * 6,
        out_specs=(pl.BlockSpec(memory_space=pltpu.VMEM),) * 2,
        scratch_shapes=[
            pltpu.VMEM((cols, WIDTH), jnp.bfloat16),
            pltpu.VMEM((CLASSES, 2 * WIDTH), jnp.bfloat16),
            pltpu.VMEM((ROT * CLASSES, cols), jnp.float32),
            pltpu.VMEM((ROT * CLASSES, cols), jnp.bfloat16),
            pltpu.VMEM((CLASSES, 2 * WIDTH), jnp.float32),
        ],
        compiler_params=pltpu.CompilerParams(vmem_limit_bytes=60 * 2**20),
        name="em_step",
    )(
        refs_angle,
        images_angle,
        jnp.tile(filter_weight, (1, repeats)),
        cos_flat,
        sin_flat,
        weight_rows,
    )


def on_device(images, class_refs, sigma2, ctf_group, defocus_bin):
    width = 2 * SHELLS * ANG
    whole_refs = lax.all_gather(class_refs, "img", axis=1, tiled=True)
    refs_angle = angle_major(whole_refs)
    filter_weight, shell_weight = image_weights(ctf_group, defocus_bin, sigma2)
    numerator, field = em_step(refs_angle, angle_major(images), filter_weight, shell_weight)
    numerator = shell_major(numerator)
    local_weights = field[:, :SHELLS]
    share_cols = width // lax.axis_size("img")
    offset = lax.axis_index("img") * share_cols
    numerator_share = lax.psum_scatter(numerator, "img", scatter_dimension=1, tiled=True)
    weights = lax.psum(local_weights, "img")
    weight_field = jnp.broadcast_to(weights[:, None, :, None], (CLASSES, 2, SHELLS, ANG)).reshape(
        CLASSES, width
    )
    field_share = lax.dynamic_slice_in_dim(weight_field, offset, share_cols, 1)
    return numerator_share / (field_share + 1.0)


def solution(mesh):
    in_specs = (
        P(("groups", "img"), None),
        P("groups", "img"),
        P("groups", None),
        P(("groups", "img")),
        P(("groups", "img")),
    )
    out_specs = P("groups", "img")
    return jax.shard_map(
        on_device, mesh=mesh, in_specs=in_specs, out_specs=out_specs, check_vma=False
    )
```

profile of v0, /device:TPU:0, one launch (start us, length us, event | category | flops | bytes accessed | tf_op | source)
XLA Modules:
  0.0 153.8 jit_solution(5105886894785399455)
XLA Ops:
  6.5 0.0 copy-start
  6.5 0.0 reduce-scatter.4.cloned.1.call-start
  6.6 0.1 broadcast_in_dim.10
  6.7 0.1 mul.193
  6.8 0.1 mul.197
  6.9 0.1 multiply_add_fusion
  7.0 4.2 %fusion = (f32[49,144,1,16]{0,3,2,1:T(8,128)S(1)}, f32[49,144,1,16]{0,3,2,1:T(8,128)S(1)}, f32[49,144,1,16]{0,3,2,1:T(8,128)S(1)}) fusion(f32[49,144]{0,1:T(8,128)S(1)} %multiply_add_fusion, f32[16]{0:T(128)S(1)} %fusion.14), kind=kLoop, calls=%fused_computation.4 | loop fusion | flops 225792 | bytes 1383040 | tf_op jit(solution)/shard_map/neg | solution.py:62
  11.2 0.2 pad_maximum_fusion.1
  11.3 1.7 %copy.32.refs_4_ = f32[49,4608]{1,0:T(8,128)} copy(f32[49,4608]{0,1:T(8,128)S(1)} %bitcast.29) | data formatting | bytes 1806336 | tf_op jit(solution)/shard_map/reshape | solution.py:62
  13.1 0.2 pad_maximum_fusion
  13.3 0.0 copy-start.4
  13.3 0.0 copy-start.5
  13.3 1.8 %copy.31.refs_3_ = f32[49,4608]{1,0:T(8,128)} copy(f32[49,4608]{0,1:T(8,128)S(1)} %bitcast.30) | data formatting | bytes 1806336 | tf_op jit(solution)/shard_map/reshape | solution.py:61
  15.1 0.0 copy-done.4
  15.1 0.3 fusion.1
  15.3 0.0 copy-done
  15.3 0.0 copy-done.5
  15.3 0.2 divide_bitcast_fusion
  15.5 0.2 tile.33
  15.7 0.0 copy-start.2
  15.8 0.4 tile.34
  16.2 0.1 copy.29
  16.3 0.7 tile.31.refs_2_
  17.0 0.0 copy-done.2
  17.0 25.0 %all-gather = bf16[16,288,48]{1,2,0:T(8,128)(2,1)S(1)} all-gather(bf16[1,288,48]{1,2,0:T(8,128)(2,1)S(1)} %bitcast.37), channel_id=1, replica_groups=mesh['groups'=2,'img'=16] {'img'}, dimensions={0}, use_global_device_ids=true | all-gather | bytes 470016 | tf_op jit(solution)/shard_map/all_gather | solution.py:269
  42.0 0.1 copy.26
  42.2 0.6 reshape.163
  42.7 1.4 reshape.153
  44.1 1.7 %copy.27 = bf16[48,144,2,16]{0,3,2,1:T(8,128)(2,1)S(1)} copy(bf16[48,144,2,16]{1,3,2,0:T(8,128)(2,1)S(1)} %bitcast.33) | data formatting | bytes 884736 | tf_op jit(solution)/shard_map/transpose | solution.py:33
  45.8 0.0 copy-start.1
  45.8 1.2 copy.30.refs_0_
  47.1 0.0 copy-done.1
  47.1 0.2 reshape.155
  47.3 0.5 copy.28
  47.8 1.5 reshape.156.refs_1_
  49.3 0.7 pad.4.refs_5_
  50.0 29.7 %em_step.1 = (f32[48,4608]{1,0:T(8,128)}, f32[48,128]{1,0:T(8,128)}) custom-call(bf16[48,4608]{1,0:T(8,128)(2,1)} %copy.30.refs_0_, bf16[8,4608]{1,0:T(8,128)(2,1)} %reshape.156.refs_1_, f32[8,128]{1,0:T(8,128)} %tile.31.refs_2_, f32[49,4608]{1,0:T(8,128)} %copy.31.refs_3_, f32[49,4608]{1,0:T(8,128)} %copy.32.refs_4_, f32[128,512]{1,0:T(8,128)} %pad.4.refs_5_), custom_call_target="tpu_custom_call" | custom-call | tf_op jit(solution)/shard_map/em_step/pallas_call | solution.py:240
  79.8 1.8 %copy.33 = f32[48,4608]{0,1:T(8,128)S(1)} copy(f32[48,4608]{1,0:T(8,128)} %get-tuple-element.7) | data formatting | bytes 1769472 | tf_op jit(solution)/shard_map/em_step/pallas_call | solution.py:240
  81.5 2.8 %copy.37 = f32[48,2,16,144]{0,3,2,1:T(8,128)} copy(f32[48,2,16,144]{0,2,1,3:T(8,128)S(1)} %bitcast.31) | data formatting | bytes 1769472
  84.3 0.0 copy-start.3
  84.3 0.0 reduce-scatter.4.cloned.1.call-update
  84.3 0.7 copy-done.3
  85.1 58.3 %psum.7 = f32[48,16]{1,0:T(8,128)S(1)} all-reduce(f32[48,16]{1,0:T(8,128)S(1)} %bitcast.38), channel_id=1, replica_groups=mesh['groups'=2,'img'=16] {'img'}, use_global_device_ids=true, to_apply=%region_1.2 | all-reduce | flops 768 | bytes 6144 | tf_op jit(solution)/shard_map/psum | solution.py:278
  143.3 0.2 broadcast_in_dim.11
  143.5 1.0 reshape.161
  144.5 0.7 reduce-scatter.4.cloned.1.call-done
  145.2 1.0 copy.36
  146.2 0.7 add_divide_fusion
  (7 shorter events, 0.1 us)
Async XLA Ops:
  6.5 8.8 %copy-start = (f32[16,16]{1,0:T(8,128)S(1)}, f32[16,16]{1,0:T(8,128)}, u32[]{:S(2)}) copy-start(f32[16,16]{1,0:T(8,128)} %param.7) | copy-start | bytes 3076
  6.5 138.7 %reduce-scatter.4.cloned.1.call-start = ((), (), s32[]{:S(2)}) async-start(), calls=%async_computation.1 | async-start | bytes 2506752
  13.3 1.8 %copy-start.4 = (s32[8]{0:T(128)S(1)}, s32[8]{0:T(128)}, u32[]{:S(2)}) copy-start(s32[8]{0:T(128)} %param.9) | copy-start | bytes 100
  13.3 2.0 %copy-start.5 = (s32[8]{0:T(128)S(1)}, s32[8]{0:T(128)}, u32[]{:S(2)}) copy-start(s32[8]{0:T(128)} %param.8) | copy-start | bytes 100
  15.7 1.3 copy-start.2
  45.8 1.3 copy-start.1
  84.3 0.7 copy-start.3
Sparse Core Ops, SparseCore 0:
  84.5 60.7 reduce-scatter.3
where the time goes:
time: 154 us
  blocking collectives  83.3 us (54%)
  Pallas kernels  29.7 us (19%)
  local copies, waits for them, and re-layouts  20.6 us (13%)
  between operations  13.6 us (9%)
  other arithmetic  5.49 us (4%)
    psum x1, blocking collectives, on_device(): weights = lax.psum(local_weights, 'img')  58.3 us
    pallas_call x1, Pallas kernels, em_step(): pl.pallas_call(lambda *refs: em_kernel(count_img, *refs), out_shape=(jax....  29.7 us
    all_gather x1, blocking collectives, on_device(): whole_refs = lax.all_gather(class_refs, 'img', axis=1, tiled=True)  25 us
    unnamed x15, local copies, waits for them, and re-layouts  5.09 us
    reshape x5, local copies, waits for them, and re-layouts, angle_major(): values.reshape(count, 2, SHELLS, ANG).transpose(0, 3, 1, 2)  4.83 us
    neg x1, other arithmetic, phase_flat(): -sine_table  4.18 us
  transfers between devices with their start and end apart: 1, of which 1 were waited for; matrix products, arithmetic and copies ran while one was open for 1% of the time, Pallas kernels for 0%

commit v1 on v0

v1 whole, which is shorter than its diff:
```python
import math

import jax
import jax.numpy as jnp
import numpy as np
from jax import lax
from jax.experimental import pallas as pl
from jax.experimental.pallas import tpu as pltpu
from jax.sharding import PartitionSpec as P

CLASSES = 48
ROT = 36
SHELLS = 16
ANG = 144
REACH = 3
SHIFTS = 49
BINS = 32
NGROUP = 16


def shell_radius():
    return (jnp.arange(SHELLS, dtype=jnp.float32) + 1.0) / (2.0 * SHELLS)


def ctf_table():
    defocus = 1.0 + jnp.arange(BINS, dtype=jnp.float32) / BINS
    radius = shell_radius()
    return -jnp.sin(80.0 * defocus[:, None] * radius[None, :] ** 2 + 0.1)


def image_weights(ctf_group, defocus_bin, sigma2):
    bin_hot = (defocus_bin[:, None] == jnp.arange(BINS, dtype=jnp.int32)[None, :]).astype(
        jnp.float32
    )
    group_hot = (ctf_group[:, None] == jnp.arange(NGROUP, dtype=jnp.int32)[None, :]).astype(
        jnp.float32
    )
    ctf_sel = jnp.dot(bin_hot, ctf_table(), precision=lax.Precision.HIGHEST)
    noise_sel = jnp.dot(group_hot, sigma2, precision=lax.Precision.HIGHEST)
    return (ctf_sel / noise_sel, ctf_sel * ctf_sel / noise_sel)


LANES = 128
PARTS = 2 * SHELLS
SPAN = ANG // ROT * PARTS
WIDTH = ROT * SPAN
SIDE = 2 * REACH + 1
SLOTS = SIDE + 1
BIG = 1e30


def phase_parts():
    offsets = np.arange(SIDE) - REACH
    angles = 2.0 * np.pi * np.arange(ANG) / ANG
    radius = (np.arange(SHELLS) + 1.0) / (2.0 * SHELLS)
    tables = []
    for direction in (np.cos(angles), np.sin(angles)):
        phase = 2.0 * np.pi * offsets[:, None, None] * direction[None, :, None] * radius
        cosine, sine = np.cos(phase), np.sin(phase)
        tables.append(np.stack([cosine, cosine], axis=2).reshape(SIDE, WIDTH))
        tables.append(np.stack([-sine, sine], axis=2).reshape(SIDE, WIDTH))
    return np.stack(tables).astype(np.float32)


def fold_lanes(row, count_img, combine):
    cols = row.shape[1]
    total = row[:, :LANES]
    for start in range(LANES, cols, LANES):
        total = combine(total, row[:, start : start + LANES])
    reach = count_img
    while reach < LANES:
        total = combine(total, pltpu.roll(total, reach, 1))
        reach *= 2
    return jnp.concatenate([total] * (cols // LANES), axis=1)


def em_kernel(
    count_dev,
    img_ref,
    refs_ref,
    fw_ref,
    phase_ref,
    sw_ref,
    out_ref,
    feats,
    twice,
    scores,
    post,
    acc,
    turned_img,
    turned,
    turned_field,
    partial,
    got,
    pay,
    mid,
    mixed,
    final,
    near_send,
    near_recv,
    far_send,
    far_recv,
    pair_send,
    pair_recv,
    last_send,
    last_recv,
):
    rows = CLASSES
    count_img = img_ref.shape[0]
    share = refs_ref.shape[1]
    cols = feats.shape[0]
    half = count_dev // 2
    piece = min(share, ANG)
    pieces = share // piece
    me = lax.axis_index("img")
    core = lax.rem(me, 2)
    place = lax.div(me, 2)
    partner = me + 1 - 2 * core

    def ahead(offset):
        return lax.rem(place + offset, half)

    def behind(offset):
        return lax.rem(place + half - offset, half)

    barrier = pltpu.get_barrier_semaphore()
    for offset in range(1, half):
        pl.semaphore_signal(
            barrier,
            inc=1,
            device_id={"img": 2 * ahead(offset) + core},
            device_id_type=pl.DeviceIdType.MESH,
        )
    pl.semaphore_signal(
        barrier, inc=1, device_id={"img": partner}, device_id_type=pl.DeviceIdType.MESH
    )
    pl.semaphore_wait(barrier, half)

    def remote(source, target, send, recv, device):
        return pltpu.make_async_remote_copy(
            src_ref=source,
            dst_ref=target,
            send_sem=send,
            recv_sem=recv,
            device_id={"img": device},
            device_id_type=pl.DeviceIdType.MESH,
        )

    far = [
        remote(
            refs_ref,
            got.at[me],
            far_send.at[offset],
            far_recv.at[offset],
            2 * ahead(offset) + core,
        )
        for offset in range(1, half)
    ]
    near = [remote(refs_ref, got.at[me], near_send.at[0], near_recv.at[0], partner)]
    for copy in far + near:
        copy.start()

    for part in range(PARTS):
        block = img_ref[:, part * ANG : (part + 1) * ANG].astype(jnp.float32)
        turned_img[pl.ds(part, ANG, stride=PARTS), :] = block.T
    weight = fw_ref[...]
    lane = lax.broadcasted_iota(jnp.int32, (count_img, WIDTH), 1)
    real_lane = lax.rem(lane, PARTS) < SHELLS

    def swap(value):
        return jnp.where(
            real_lane, pltpu.roll(value, WIDTH - SHELLS, 1), pltpu.roll(value, SHELLS, 1)
        )

    filtered = jnp.concatenate(
        [turned_img[q * SPAN : (q + 1) * SPAN, :].T * weight for q in range(ROT)], axis=1
    )
    partial[0] = filtered
    partial[1] = swap(filtered)
    group = SLOTS * count_img

    def feature_step(step, carry):
        moved = (
            partial[0] * phase_ref[0, pl.ds(step, 1), :]
            + partial[1] * phase_ref[1, pl.ds(step, 1), :]
        )
        partial[2] = moved
        partial[3] = swap(moved)
        start = pl.multiple_of(step * group, group)
        for slot in range(0, SLOTS, 2):
            pair = []
            for shift in (slot, slot + 1):
                if shift < SIDE:
                    pair.append(
                        partial[2] * phase_ref[2, shift : shift + 1, :]
                        + partial[3] * phase_ref[3, shift : shift + 1, :]
                    )
                else:
                    pair.append(jnp.zeros((count_img, WIDTH), jnp.float32))
            feats[pl.ds(start + slot * count_img, 2 * count_img), :] = jnp.concatenate(
                pair, axis=0
            ).astype(jnp.bfloat16)
        return carry

    lax.fori_loop(0, SIDE, feature_step, 0)
    feats[SIDE * group :, :] = jnp.zeros((cols - SIDE * group, WIDTH), jnp.bfloat16)

    def place_refs(block, source):
        block = block.astype(jnp.float32)
        for index in range(pieces):
            first = source * share + index * piece
            start = lax.rem(first, ANG) * PARTS + lax.div(first, ANG)
            turned[pl.ds(start, piece, stride=PARTS), :] = block[
                :, index * piece : (index + 1) * piece
            ].T

    for offset in range(1, half):
        source = 2 * behind(offset) + core
        far[offset - 1].wait_recv()
        copy = remote(
            got.at[source], got.at[source], near_send.at[offset], near_recv.at[offset], partner
        )
        copy.start()
        near.append(copy)
    place_refs(refs_ref[...], me)
    for offset in range(1, half):
        source = 2 * behind(offset) + core
        place_refs(got[source], source)
    for offset in range(half):
        source = 2 * behind(offset) + 1 - core
        near[offset].wait_recv()
        place_refs(got[source], source)
    for copy in far + near:
        copy.wait_send()

    power = jnp.zeros((rows, SPAN), jnp.float32)
    for q in range(ROT):
        block = turned[q * SPAN : (q + 1) * SPAN, :].T
        power = power + block * block
        block = block.astype(jnp.bfloat16)
        twice[:, q * SPAN : (q + 1) * SPAN] = block
        twice[:, WIDTH + q * SPAN : WIDTH + (q + 1) * SPAN] = block
    quad = 0.5 * lax.dot_general(
        power,
        sw_ref[...],
        (((1,), (0,)), ((), ())),
        precision=lax.Precision.HIGHEST,
        preferred_element_type=jnp.float32,
    )
    col = lax.broadcasted_iota(jnp.int32, (rows, cols), 1)
    used = (lax.rem(col, group) < SIDE * count_img) & (col < SIDE * group)
    quad = jnp.where(used, quad, BIG)

    depth = 4 * SPAN
    for turn in range(ROT):
        scores[turn * rows : (turn + 1) * rows, :] = -quad

    def cross_step(step, carry):
        base = pl.multiple_of(step * depth, depth)
        left = jnp.concatenate(
            [
                twice[:, pl.ds(pl.multiple_of(base + (ROT - turn) * SPAN, SPAN), depth)]
                for turn in range(ROT)
            ],
            axis=0,
        )
        scores[...] += lax.dot_general(
            left,
            feats[:, pl.ds(base, depth)],
            (((1,), (1,)), ((), ())),
            preferred_element_type=jnp.float32,
        )
        return carry

    lax.fori_loop(0, WIDTH // depth, cross_step, 0)

    def max_step(turn, best):
        start = pl.multiple_of(turn * rows, rows)
        return jnp.maximum(best, scores[pl.ds(start, rows), :])

    best = lax.fori_loop(0, ROT, max_step, jnp.full((rows, cols), -BIG, jnp.float32))
    top = fold_lanes(jnp.max(best, axis=0, keepdims=True), count_img, jnp.maximum)

    def exp_step(turn, total):
        start = pl.multiple_of(turn * rows, rows)
        value = jnp.exp(scores[pl.ds(start, rows), :] - top)
        scores[pl.ds(start, rows), :] = value
        return total + value

    total = lax.fori_loop(0, ROT, exp_step, jnp.zeros((rows, cols), jnp.float32))
    norm = fold_lanes(jnp.sum(total, axis=0, keepdims=True), count_img, jnp.add)
    scale = 1.0 / norm

    def post_step(turn, carry):
        start = pl.multiple_of(turn * rows, rows)
        post[pl.ds(start, rows), :] = (scores[pl.ds(start, rows), :] * scale).astype(jnp.bfloat16)
        return carry

    lax.fori_loop(0, ROT, post_step, 0)
    turned_field[...] = lax.dot_general(
        total * scale,
        sw_ref[...],
        (((1,), (1,)), ((), ())),
        precision=lax.Precision.HIGHEST,
        preferred_element_type=jnp.float32,
    ).T

    acc[...] = jnp.zeros_like(acc)
    wide = 2 * SPAN

    def back_step(step, carry):
        base = pl.multiple_of(step * wide, wide)
        oriented = jnp.dot(
            post[...], feats[:, pl.ds(base, wide)], preferred_element_type=jnp.float32
        )
        for turn in range(ROT):
            where = pl.ds(pl.multiple_of(base + (ROT - turn) * SPAN, SPAN), wide)
            acc[:, where] += oriented[turn * rows : (turn + 1) * rows]
        return carry

    lax.fori_loop(0, WIDTH // wide, back_step, 0)
    for q in range(ROT):
        low = acc[:, q * SPAN : (q + 1) * SPAN]
        turned[q * SPAN : (q + 1) * SPAN, :] = (
            low + acc[:, WIDTH + q * SPAN : WIDTH + (q + 1) * SPAN]
        ).T

    def block_for(device):
        parts, weights = [], []
        for index in range(pieces):
            first = device * share + index * piece
            part = lax.div(first, ANG)
            start = lax.rem(first, ANG) * PARTS + part
            parts.append(turned[pl.ds(start, piece, stride=PARTS), :])
            value = turned_field[pl.ds(lax.rem(part, SHELLS), 1), :]
            high = value.astype(jnp.bfloat16).astype(jnp.float32)
            weights += [high, value - high]
        extra = pay.shape[2] - share - len(weights)
        weights.append(jnp.zeros((extra, rows), jnp.float32))
        return jnp.concatenate(parts + weights, axis=0).T.astype(jnp.bfloat16)

    pairs = []
    for offset in [*range(1, half), 0]:
        slot = ahead(offset)
        pay[offset] = block_for(2 * slot + 1 - core)
        copy = remote(
            pay.at[offset], mid.at[offset], pair_send.at[offset], pair_recv.at[offset], partner
        )
        copy.start()
        pairs.append(copy)
    for offset in range(half):
        pay[half + offset] = block_for(2 * ahead(offset) + core)

    lasts = []
    for index, offset in enumerate([*range(1, half), 0]):
        pairs[index].wait_recv()
        value = pay[half + offset].astype(jnp.float32) + mid[offset].astype(jnp.float32)
        if offset:
            lead = value[:, :share]
            tail = value[:, share:]
            mixed[offset, :, :share] = lead.astype(jnp.bfloat16)
            mixed[offset, :, share:] = tail.astype(jnp.bfloat16)
            copy = remote(
                mixed.at[offset],
                final.at[offset],
                last_send.at[offset],
                last_recv.at[offset],
                2 * ahead(offset) + core,
            )
            copy.start()
            lasts.append(copy)
        else:
            result = value
    for index, copy in enumerate(lasts):
        copy.wait_recv()
        result = result + final[index + 1].astype(jnp.float32)
    for index in range(pieces):
        place_w = share + 2 * index
        weights = result[:, place_w : place_w + 1] + result[:, place_w + 1 : place_w + 2]
        out_ref[:, index * piece : (index + 1) * piece] = result[
            :, index * piece : (index + 1) * piece
        ] / (weights + 1.0)
    for copy in pairs + lasts:
        copy.wait_send()


def on_device(images, class_refs, sigma2, ctf_group, defocus_bin):
    count_dev = lax.axis_size("img")
    half = count_dev // 2
    count_img = images.shape[0]
    share = class_refs.shape[1]
    cols = -(-SIDE * SLOTS * count_img // LANES) * LANES
    repeats = SPAN // SHELLS
    filter_weight, shell_weight = image_weights(ctf_group, defocus_bin, sigma2)
    packed = share + 8
    return pl.pallas_call(
        lambda *refs: em_kernel(count_dev, *refs),
        out_shape=jax.ShapeDtypeStruct(class_refs.shape, jnp.float32),
        in_specs=[pl.BlockSpec(memory_space=pltpu.VMEM)] * 5,
        out_specs=pl.BlockSpec(memory_space=pltpu.VMEM),
        scratch_shapes=[
            pltpu.VMEM((cols, WIDTH), jnp.bfloat16),
            pltpu.VMEM((CLASSES, 2 * WIDTH), jnp.bfloat16),
            pltpu.VMEM((ROT * CLASSES, cols), jnp.float32),
            pltpu.VMEM((ROT * CLASSES, cols), jnp.bfloat16),
            pltpu.VMEM((CLASSES, 2 * WIDTH), jnp.float32),
            pltpu.VMEM((WIDTH, count_img), jnp.float32),
            pltpu.VMEM((WIDTH, CLASSES), jnp.float32),
            pltpu.VMEM((SPAN, CLASSES), jnp.float32),
            pltpu.VMEM((4, count_img, WIDTH), jnp.float32),
            pltpu.VMEM((count_dev, CLASSES, share), jnp.bfloat16),
            pltpu.VMEM((count_dev, CLASSES, packed), jnp.bfloat16),
            pltpu.VMEM((half, CLASSES, packed), jnp.bfloat16),
            pltpu.VMEM((half, CLASSES, packed), jnp.bfloat16),
            pltpu.VMEM((half, CLASSES, packed), jnp.bfloat16),
        ]
        + [pltpu.SemaphoreType.DMA((half,))] * 8,
        compiler_params=pltpu.CompilerParams(
            vmem_limit_bytes=60 * 2**20, collective_id=0, has_side_effects=True
        ),
        name="em_step",
    )(
        images,
        class_refs,
        jnp.tile(filter_weight, (1, repeats)),
        jnp.asarray(phase_parts()),
        jnp.tile(shell_weight.T, (repeats, cols // count_img)),
    )


def solution(mesh):
    in_specs = (
        P(("groups", "img"), None),
        P("groups", "img"),
        P("groups", None),
        P(("groups", "img")),
        P(("groups", "img")),
    )
    out_specs = P("groups", "img")
    return jax.shard_map(
        on_device, mesh=mesh, in_specs=in_specs, out_specs=out_specs, check_vma=False
    )
```

time: 154 us -> 60.3 us (0.39)
  blocking collectives: 83.3 us -> 0 us
  Pallas kernels: 29.7 us -> 54.4 us
  local copies, waits for them, and re-layouts: 20.6 us -> 3.84 us
  between operations: 13.6 us -> 0.03 us
  other arithmetic: 5.49 us -> 0.02 us
    psum x1 -> x0, blocking collectives: 58.3 us -> none  [on_device(): weights = lax.psum(local_weights, 'img')]
    all_gather x1 -> x0, blocking collectives: 25 us -> none  [on_device(): whole_refs = lax.all_gather(class_refs, 'img', axis=1, tiled=True)]
    pallas_call x1, Pallas kernels: 29.7 us -> 54.4 us  [on_device(): pl.pallas_call(lambda *refs: em_kernel(count_dev, *refs), out_shape=jax.S...]
    reshape x8 -> x0, local copies, waits for them, and re-layouts: 9.33 us -> none  [the longest x5 4.83 us: angle_major(): values.reshape(count, 2, SHELLS, ANG).transpose(0, 3, 1, 2)]
    neg x1 -> x0, other arithmetic: 4.18 us -> none  [phase_flat(): -sine_table]
    unnamed x15 -> x3, local copies, waits for them, and re-layouts: 5.09 us -> 1.53 us
    pallas_call x1 -> x0, local copies, waits for them, and re-layouts: 1.77 us -> none  [em_step(): pl.pallas_call(lambda *refs: em_kernel(count_img, *refs), out_shape=(jax....]
    transpose x1 -> x0, local copies, waits for them, and re-layouts: 1.71 us -> none  [angle_major(): values.reshape(count, 2, SHELLS, ANG).transpose(0, 3, 1, 2)]
  transfers between devices with their start and end apart: 1 -> 0, of which waited for: 1 -> 0; matrix products, arithmetic and copies ran while one was open for 1% -> 0% of each run, Pallas kernels for 0% -> 0%
where the time goes in v1:
time: 60.3 us; the launch traced here: 60 us
  Pallas kernels  54.4 us (90%)
  local copies, waits for them, and re-layouts  3.84 us (6%)
  matrix products  1.76 us (3%)
    pallas_call x1, Pallas kernels, on_device(): pl.pallas_call(lambda *refs: em_kernel(count_dev, *refs), out_shape=jax.S...  54.4 us
    another operation x3, local copies, waits for them, and re-layouts, on_device(): jnp.tile(shell_weight.T, (repeats, cols // count_img))  1.62 us
    unnamed x3, local copies, waits for them, and re-layouts  1.53 us

profile of v1, /device:TPU:0, one launch (start us, length us, event | category | flops | bytes accessed | tf_op | source)
XLA Modules:
  0.0 60.0 jit_solution(2830609368853447887)
XLA Ops:
  0.0 0.0 copy-start
  0.0 0.9 %fusion = f32[8,16]{1,0:T(8,128)S(1)} fusion(f32[16]{0:T(128)S(1)} %multiply_multiply_fusion, f32[32]{0:T(128)S(1)} %add_multiply_fusion, s32[8]{0:T(128)} %param.10), kind=kOutput, calls=%fused_computation | convolution fusion | flops 50944 | bytes 736 | tf_op jit(solution)/shard_map/dot_general | solution.py:38
  0.9 0.0 copy-done
  0.9 0.9 %divide_bitcast_fusion = (f32[16,8]{0,1:T(8,128)S(1)}, f32[8,16]{1,0:T(8,128)S(1)}) fusion(f32[8,16]{1,0:T(8,128)S(1)} %fusion, f32[16,16]{1,0:T(8,128)S(1)} %copy-done, s32[8]{0:T(128)} %param.9), kind=kOutput, calls=%fused_computation.8 | convolution fusion | flops 25088 | bytes 2592 | tf_op jit(solution)/shard_map/dot_general | solution.py:39
  1.8 0.7 %tile.9.refs_2_ = f32[8,128]{1,0:T(8,128)} reshape(f32[8,8,16]{2,1,0:T(8,128)S(1)} %tile.8) | data formatting | bytes 8192 | tf_op jit(solution)/shard_map/tile | solution.py:425
  2.5 0.2 tile.20
  2.7 0.6 tile.21
  3.3 0.8 %copy.8.refs_4_ = f32[128,512]{1,0:T(8,128)} copy(f32[128,512]{0,1:T(8,128)S(1)} %tile.21) | data formatting | bytes 524288 | tf_op jit(solution)/shard_map/tile | solution.py:427
  4.1 54.4 %em_step.1 = f32[48,288]{1,0:T(8,128)} custom-call(bf16[8,4608]{1,0:T(8,128)(2,1)} %refs_0_.1, bf16[48,288]{1,0:T(8,128)(2,1)} %refs_1_.1, f32[8,128]{1,0:T(8,128)} %tile.9.refs_2_, f32[4,7,4608]{2,1,0:T(8,128)} %constant.14.clone.refs_3_, f32[128,512]{1,0:T(8,128)} %copy.8.refs_4_), custom_call_target="tpu_custom_call" | custom-call | tf_op jit(solution)/shard_map/em_step/pallas_call | solution.py:396
  58.5 1.5 %copy.10 = f32[48,288]{1,0:T(8,128)} copy(f32[48,288]{1,0:T(8,128)} %em_step.1) | data formatting | bytes 110592
  (3 shorter events, 0.0 us)
Async XLA Ops:
  0.0 0.9 %copy-start = (f32[16,16]{1,0:T(8,128)S(1)}, f32[16,16]{1,0:T(8,128)}, u32[]{:S(2)}) copy-start(f32[16,16]{1,0:T(8,128)} %param.8) | copy-start | bytes 3076

commit v2 on v1

--- a/solution.py
+++ b/solution.py
@@ -16,28 +16,6 @@
 SHIFTS = 49
 BINS = 32
 NGROUP = 16
-
-
-def shell_radius():
-    return (jnp.arange(SHELLS, dtype=jnp.float32) + 1.0) / (2.0 * SHELLS)
-
-
-def ctf_table():
-    defocus = 1.0 + jnp.arange(BINS, dtype=jnp.float32) / BINS
-    radius = shell_radius()
-    return -jnp.sin(80.0 * defocus[:, None] * radius[None, :] ** 2 + 0.1)
-
-
-def image_weights(ctf_group, defocus_bin, sigma2):
-    bin_hot = (defocus_bin[:, None] == jnp.arange(BINS, dtype=jnp.int32)[None, :]).astype(
-        jnp.float32
-    )
-    group_hot = (ctf_group[:, None] == jnp.arange(NGROUP, dtype=jnp.int32)[None, :]).astype(
-        jnp.float32
-    )
-    ctf_sel = jnp.dot(bin_hot, ctf_table(), precision=lax.Precision.HIGHEST)
-    noise_sel = jnp.dot(group_hot, sigma2, precision=lax.Precision.HIGHEST)
-    return (ctf_sel / noise_sel, ctf_sel * ctf_sel / noise_sel)
 
 
 LANES = 128
@@ -62,6 +40,13 @@
     return np.stack(tables).astype(np.float32)
 
 
+def ctf_lanes():
+    radius = (np.arange(SHELLS) + 1.0) / (2.0 * SHELLS)
+    defocus = 1.0 + np.arange(BINS) / BINS
+    table = -np.sin(80.0 * defocus[:, None] * radius**2 + 0.1)
+    return np.tile(table, (1, SPAN // SHELLS)).astype(np.float32)
+
+
 def fold_lanes(row, count_img, combine):
     cols = row.shape[1]
     total = row[:, :LANES]
@@ -78,9 +63,11 @@
     count_dev,
     img_ref,
     refs_ref,
-    fw_ref,
+    sigma_ref,
+    group_ref,
+    bin_ref,
+    ctf_ref,
     phase_ref,
-    sw_ref,
     out_ref,
     feats,
     twice,
@@ -90,6 +77,7 @@
     turned_img,
     turned,
     turned_field,
+    sw_ref,
     partial,
     got,
     pay,
@@ -163,7 +151,31 @@
     for part in range(PARTS):
         block = img_ref[:, part * ANG : (part + 1) * ANG].astype(jnp.float32)
         turned_img[pl.ds(part, ANG, stride=PARTS), :] = block.T
-    weight = fw_ref[...]
+    repeats = SPAN // SHELLS
+    noise = jnp.concatenate([sigma_ref[...]] * repeats, axis=1)
+
+    def pick(ids, table):
+        hot = ids == lax.broadcasted_iota(jnp.int32, (table.shape[0], count_img), 0)
+        return lax.dot_general(
+            hot.astype(jnp.float32),
+            table,
+            (((0,), (0,)), ((), ())),
+            precision=lax.Precision.HIGHEST,
+            preferred_element_type=jnp.float32,
+        )
+
+    ctf = pick(bin_ref[...], ctf_ref[...])
+    noise = pick(group_ref[...], noise)
+    weight = ctf / noise
+    image_col = lax.rem(lax.broadcasted_iota(jnp.int32, (count_img, cols), 1), count_img)
+    image_hot = image_col == lax.broadcasted_iota(jnp.int32, (count_img, cols), 0)
+    sw_ref[...] = lax.dot_general(
+        ctf * ctf / noise,
+        image_hot.astype(jnp.float32),
+        (((0,), (0,)), ((), ())),
+        precision=lax.Precision.HIGHEST,
+        preferred_element_type=jnp.float32,
+    )
     lane = lax.broadcasted_iota(jnp.int32, (count_img, WIDTH), 1)
     real_lane = lax.rem(lane, PARTS) < SHELLS
 
@@ -214,6 +226,7 @@
                 :, index * piece : (index + 1) * piece
             ].T
 
+    place_refs(refs_ref[...], me)
     for offset in range(1, half):
         source = 2 * behind(offset) + core
         far[offset - 1].wait_recv()
@@ -222,9 +235,6 @@
         )
         copy.start()
         near.append(copy)
-    place_refs(refs_ref[...], me)
-    for offset in range(1, half):
-        source = 2 * behind(offset) + core
         place_refs(got[source], source)
     for offset in range(half):
         source = 2 * behind(offset) + 1 - core
@@ -337,29 +347,25 @@
             weights += [high, value - high]
         extra = pay.shape[2] - share - len(weights)
         weights.append(jnp.zeros((extra, rows), jnp.float32))
-        return jnp.concatenate(parts + weights, axis=0).T.astype(jnp.bfloat16)
+        return jnp.concatenate(parts + weights, axis=0).T
 
     pairs = []
     for offset in [*range(1, half), 0]:
         slot = ahead(offset)
-        pay[offset] = block_for(2 * slot + 1 - core)
+        pay[offset] = block_for(2 * slot + 1 - core).astype(jnp.bfloat16)
         copy = remote(
             pay.at[offset], mid.at[offset], pair_send.at[offset], pair_recv.at[offset], partner
         )
         copy.start()
         pairs.append(copy)
-    for offset in range(half):
-        pay[half + offset] = block_for(2 * ahead(offset) + core)
 
     lasts = []
     for index, offset in enumerate([*range(1, half), 0]):
+        own = block_for(2 * ahead(offset) + core)
         pairs[index].wait_recv()
-        value = pay[half + offset].astype(jnp.float32) + mid[offset].astype(jnp.float32)
+        value = own + mid[offset].astype(jnp.float32)
         if offset:
-            lead = value[:, :share]
-            tail = value[:, share:]
-            mixed[offset, :, :share] = lead.astype(jnp.bfloat16)
-            mixed[offset, :, share:] = tail.astype(jnp.bfloat16)
+            mixed[offset] = value.astype(jnp.bfloat16)
             copy = remote(
                 mixed.at[offset],
                 final.at[offset],
@@ -390,13 +396,11 @@
     count_img = images.shape[0]
     share = class_refs.shape[1]
     cols = -(-SIDE * SLOTS * count_img // LANES) * LANES
-    repeats = SPAN // SHELLS
-    filter_weight, shell_weight = image_weights(ctf_group, defocus_bin, sigma2)
     packed = share + 8
     return pl.pallas_call(
         lambda *refs: em_kernel(count_dev, *refs),
         out_shape=jax.ShapeDtypeStruct(class_refs.shape, jnp.float32),
-        in_specs=[pl.BlockSpec(memory_space=pltpu.VMEM)] * 5,
+        in_specs=[pl.BlockSpec(memory_space=pltpu.VMEM)] * 7,
         out_specs=pl.BlockSpec(memory_space=pltpu.VMEM),
         scratch_shapes=[
             pltpu.VMEM((cols, WIDTH), jnp.bfloat16),
@@ -407,9 +411,10 @@
             pltpu.VMEM((WIDTH, count_img), jnp.float32),
             pltpu.VMEM((WIDTH, CLASSES), jnp.float32),
             pltpu.VMEM((SPAN, CLASSES), jnp.float32),
+            pltpu.VMEM((SPAN, cols), jnp.float32),
             pltpu.VMEM((4, count_img, WIDTH), jnp.float32),
             pltpu.VMEM((count_dev, CLASSES, share), jnp.bfloat16),
-            pltpu.VMEM((count_dev, CLASSES, packed), jnp.bfloat16),
+            pltpu.VMEM((half, CLASSES, packed), jnp.bfloat16),
             pltpu.VMEM((half, CLASSES, packed), jnp.bfloat16),
             pltpu.VMEM((half, CLASSES, packed), jnp.bfloat16),
             pltpu.VMEM((half, CLASSES, packed), jnp.bfloat16),
@@ -422,9 +427,11 @@
     )(
         images,
         class_refs,
-        jnp.tile(filter_weight, (1, repeats)),
+        sigma2,
+        ctf_group.reshape(1, count_img),
+        defocus_bin.reshape(1, count_img),
+        jnp.asarray(ctf_lanes()),
         jnp.asarray(phase_parts()),
-        jnp.tile(shell_weight.T, (repeats, cols // count_img)),
     )
 
 

time: 60.3 us -> 54.7 us (0.907)
  local copies, waits for them, and re-layouts: 3.84 us -> 1.52 us
  matrix products: 1.76 us -> 0 us
  Pallas kernels: 54.4 us -> 53 us
    another operation x5 -> x0, local copies, waits for them, and re-layouts: 2.31 us -> none  [the longest x3 1.62 us: on_device(): jnp.tile(shell_weight.T, (repeats, cols // count_img))]
    dot_general x2 -> x0, matrix products: 1.76 us -> none  [the longest x1 0.91 us: image_weights(): ctf_sel = jnp.dot(bin_hot, ctf_table(), precision=lax.Precision.HIGHEST)]
    pallas_call x1, Pallas kernels: 54.4 us -> 53 us  [on_device(): pl.pallas_call(lambda *refs: em_kernel(count_dev, *refs), out_shape=jax.S...]
    unnamed x3 -> x1, local copies, waits for them, and re-layouts: 1.53 us -> 1.52 us
where the time goes in v2:
time: 54.7 us; the launch traced here: 54.5 us
  Pallas kernels  53 us (97%)
  local copies, waits for them, and re-layouts  1.52 us (3%)
    pallas_call x1, Pallas kernels, on_device(): pl.pallas_call(lambda *refs: em_kernel(count_dev, *refs), out_shape=jax.S...  53 us
    unnamed x1, local copies, waits for them, and re-layouts  1.52 us

profile of v2, /device:TPU:0, one launch (start us, length us, event | category | flops | bytes accessed | tf_op | source)
XLA Modules:
  0.0 54.5 jit_solution(4064824362829449471)
XLA Ops:
  0.0 53.0 %em_step.1 = f32[48,288]{1,0:T(8,128)} custom-call(bf16[8,4608]{1,0:T(8,128)(2,1)} %refs_0_.1, bf16[48,288]{1,0:T(8,128)(2,1)} %refs_1_.1, f32[16,16]{1,0:T(8,128)} %refs_2_.1, s32[1,8]{1,0:T(1,128)} %bitcast.2, s32[1,8]{1,0:T(1,128)} %bitcast.3, f32[32,128]{1,0:T(8,128)} %constant.4.clone.refs_5_, f32[4,7,4608]{2,1,0:T(8,128)} %constant.5.clone.refs_6_), custom_call_target="tpu_custom_call" | custom-call | tf_op jit(solution)/shard_map/em_step/pallas_call | solution.py:400
  53.0 1.5 %copy.9 = f32[48,288]{1,0:T(8,128)} copy(f32[48,288]{1,0:T(8,128)} %em_step.1) | data formatting | bytes 110592

commit v3 on v2

--- a/solution.py
+++ b/solution.py
@@ -57,6 +57,44 @@
         total = combine(total, pltpu.roll(total, reach, 1))
         reach *= 2
     return jnp.concatenate([total] * (cols // LANES), axis=1)
+
+
+def packing(width):
+    full, tail = width // LANES, width % LANES
+    groups = 3 if tail and 3 * tail <= LANES and CLASSES % 48 == 0 else 1
+    return full, tail, groups
+
+
+def packed_rows(width):
+    full, tail, groups = packing(width)
+    return full * CLASSES + (CLASSES // groups if tail else 0)
+
+
+def pack(block):
+    full, tail, groups = packing(block.shape[1])
+    columns = [block[:, index * LANES : (index + 1) * LANES] for index in range(full)]
+    if tail:
+        rest = block[:, full * LANES :]
+        size = CLASSES // groups
+        pieces = [rest[index * size : (index + 1) * size] for index in range(groups)]
+        spare = LANES - groups * tail
+        if spare:
+            pieces.append(jnp.zeros((size, spare), block.dtype))
+        columns.append(jnp.concatenate(pieces, axis=1))
+    return jnp.concatenate(columns, axis=0)
+
+
+def unpack(block, width):
+    full, tail, groups = packing(width)
+    columns = [block[index * CLASSES : (index + 1) * CLASSES] for index in range(full)]
+    if tail:
+        rest = block[full * CLASSES :]
+        columns.append(
+            jnp.concatenate(
+                [rest[:, index * tail : (index + 1) * tail] for index in range(groups)], axis=0
+            )
+        )
+    return jnp.concatenate(columns, axis=1)
 
 
 def em_kernel(
@@ -79,6 +117,7 @@
     turned_field,
     sw_ref,
     partial,
+    mine,
     got,
     pay,
     mid,
@@ -98,6 +137,7 @@
     share = refs_ref.shape[1]
     cols = feats.shape[0]
     half = count_dev // 2
+    packed = share + 8
     piece = min(share, ANG)
     pieces = share // piece
     me = lax.axis_index("img")
@@ -134,9 +174,11 @@
             device_id_type=pl.DeviceIdType.MESH,
         )
 
+    mine[...] = pack(refs_ref[...].astype(jnp.float32)).astype(jnp.bfloat16)
+
     far = [
         remote(
-            refs_ref,
+            mine,
             got.at[me],
             far_send.at[offset],
             far_recv.at[offset],
@@ -144,7 +186,7 @@
         )
         for offset in range(1, half)
     ]
-    near = [remote(refs_ref, got.at[me], near_send.at[0], near_recv.at[0], partner)]
+    near = [remote(mine, got.at[me], near_send.at[0], near_recv.at[0], partner)]
     for copy in far + near:
         copy.start()
 
@@ -218,7 +260,6 @@
     feats[SIDE * group :, :] = jnp.zeros((cols - SIDE * group, WIDTH), jnp.bfloat16)
 
     def place_refs(block, source):
-        block = block.astype(jnp.float32)
         for index in range(pieces):
             first = source * share + index * piece
             start = lax.rem(first, ANG) * PARTS + lax.div(first, ANG)
@@ -226,7 +267,7 @@
                 :, index * piece : (index + 1) * piece
             ].T
 
-    place_refs(refs_ref[...], me)
+    place_refs(refs_ref[...].astype(jnp.float32), me)
     for offset in range(1, half):
         source = 2 * behind(offset) + core
         far[offset - 1].wait_recv()
@@ -235,11 +276,11 @@
         )
         copy.start()
         near.append(copy)
-        place_refs(got[source], source)
+        place_refs(unpack(got[source].astype(jnp.float32), share), source)
     for offset in range(half):
         source = 2 * behind(offset) + 1 - core
         near[offset].wait_recv()
-        place_refs(got[source], source)
+        place_refs(unpack(got[source].astype(jnp.float32), share), source)
     for copy in far + near:
         copy.wait_send()
 
@@ -345,14 +386,14 @@
             value = turned_field[pl.ds(lax.rem(part, SHELLS), 1), :]
             high = value.astype(jnp.bfloat16).astype(jnp.float32)
             weights += [high, value - high]
-        extra = pay.shape[2] - share - len(weights)
+        extra = packed - share - len(weights)
         weights.append(jnp.zeros((extra, rows), jnp.float32))
         return jnp.concatenate(parts + weights, axis=0).T
 
     pairs = []
     for offset in [*range(1, half), 0]:
         slot = ahead(offset)
-        pay[offset] = block_for(2 * slot + 1 - core).astype(jnp.bfloat16)
+        pay[offset] = pack(block_for(2 * slot + 1 - core)).astype(jnp.bfloat16)
         copy = remote(
             pay.at[offset], mid.at[offset], pair_send.at[offset], pair_recv.at[offset], partner
         )
@@ -361,7 +402,7 @@
 
     lasts = []
     for index, offset in enumerate([*range(1, half), 0]):
-        own = block_for(2 * ahead(offset) + core)
+        own = pack(block_for(2 * ahead(offset) + core))
         pairs[index].wait_recv()
         value = own + mid[offset].astype(jnp.float32)
         if offset:
@@ -380,6 +421,7 @@
     for index, copy in enumerate(lasts):
         copy.wait_recv()
         result = result + final[index + 1].astype(jnp.float32)
+    result = unpack(result, packed)
     for index in range(pieces):
         place_w = share + 2 * index
         weights = result[:, place_w : place_w + 1] + result[:, place_w + 1 : place_w + 2]
@@ -413,11 +455,12 @@
             pltpu.VMEM((SPAN, CLASSES), jnp.float32),
             pltpu.VMEM((SPAN, cols), jnp.float32),
             pltpu.VMEM((4, count_img, WIDTH), jnp.float32),
-            pltpu.VMEM((count_dev, CLASSES, share), jnp.bfloat16),
-            pltpu.VMEM((half, CLASSES, packed), jnp.bfloat16),
-            pltpu.VMEM((half, CLASSES, packed), jnp.bfloat16),
-            pltpu.VMEM((half, CLASSES, packed), jnp.bfloat16),
-            pltpu.VMEM((half, CLASSES, packed), jnp.bfloat16),
+            pltpu.VMEM((packed_rows(share), LANES), jnp.bfloat16),
+            pltpu.VMEM((count_dev, packed_rows(share), LANES), jnp.bfloat16),
+            pltpu.VMEM((half, packed_rows(packed), LANES), jnp.bfloat16),
+            pltpu.VMEM((half, packed_rows(packed), LANES), jnp.bfloat16),
+            pltpu.VMEM((half, packed_rows(packed), LANES), jnp.bfloat16),
+            pltpu.VMEM((half, packed_rows(packed), LANES), jnp.bfloat16),
         ]
         + [pltpu.SemaphoreType.DMA((half,))] * 8,
         compiler_params=pltpu.CompilerParams(

time: 54.7 us -> 53.7 us (0.982)
  Pallas kernels: 53 us -> 52 us
    pallas_call x1, Pallas kernels: 53 us -> 52 us  [on_device(): pl.pallas_call(lambda *refs: em_kernel(count_dev, *refs), out_shape=jax.S...]
where the time goes in v3:
time: 53.7 us; the launch traced here: 53.5 us
  Pallas kernels  52 us (97%)
  local copies, waits for them, and re-layouts  1.52 us (3%)
    pallas_call x1, Pallas kernels, on_device(): pl.pallas_call(lambda *refs: em_kernel(count_dev, *refs), out_shape=jax.S...  52 us
    unnamed x1, local copies, waits for them, and re-layouts  1.52 us

profile of v3, /device:TPU:0, one launch (start us, length us, event | category | flops | bytes accessed | tf_op | source)
XLA Modules:
  0.0 53.5 jit_solution(8160497492496982579)
XLA Ops:
  0.0 52.0 %em_step.1 = f32[48,288]{1,0:T(8,128)} custom-call(bf16[8,4608]{1,0:T(8,128)(2,1)} %refs_0_.1, bf16[48,288]{1,0:T(8,128)(2,1)} %refs_1_.1, f32[16,16]{1,0:T(8,128)} %refs_2_.1, s32[1,8]{1,0:T(1,128)} %bitcast.2, s32[1,8]{1,0:T(1,128)} %bitcast.3, f32[32,128]{1,0:T(8,128)} %constant.4.clone.refs_5_, f32[4,7,4608]{2,1,0:T(8,128)} %constant.5.clone.refs_6_), custom_call_target="tpu_custom_call" | custom-call | tf_op jit(solution)/shard_map/em_step/pallas_call | solution.py:442
  52.0 1.5 %copy.9 = f32[48,288]{1,0:T(8,128)} copy(f32[48,288]{1,0:T(8,128)} %em_step.1) | data formatting | bytes 110592
